TPU v7x, 512 devices: a whole 4x4x16 slice. The times are simulated.
512 devices in a mesh: fsdp: 8 (over y_lo, x), ctx: 64 (over y_hi, z, core).
Axes of the slice: x: 4, y: 4 (y_hi: 2, y_lo: 2; y = y_hi * 2 + y_lo), z: 16, core: 2. Of those that a mesh axis runs over, the one named last changes fastest.
Arguments:
- latents: float32 [8192, 64], P('ctx'), may hold values from -15 to 15
- stream: bfloat16 [8192, 3072], P('ctx'), may hold values from -6 to 6
- queries: bfloat16 [8192, 2048], P('ctx', 'fsdp'), may hold values from -200 to 200
- key_rows: bfloat16 [8192, 2048], P('ctx', 'fsdp'), may hold values from -4 to 4
- value_rows: bfloat16 [8192, 2048], P('ctx', 'fsdp'), may hold values from -6 to 6
- w_mix: bfloat16 [2048, 3072], P('fsdp', 'ctx'), may hold values from -0.25 to 0.25
- w_head: bfloat16 [3072, 128], P('fsdp'), may hold values from -0.0390625 to 0.0390625
Outputs:
- flipped: float32 [8192, 64], P('ctx')
- head_grad: float32 [3072, 128], P('fsdp')
All inputs are finite; a program needn't handle non-finite values.
Results may differ from a plain program's by a relative error of at most 0.003.
The roundings to bfloat16 on the way count: a program that leaves them out, or rounds other values in their place, can miss the bound.
Values may be sent and summed in bfloat16 or wider, within the bound.
A program may use at most 64 MiB of HBM per device.

v0:
```python
import jax
import jax.numpy as jnp
from jax import lax
from jax.sharding import PartitionSpec as P

HD = 128


def shifted(shard, axis, by):
    devices = lax.axis_size(axis)
    pairs = [(i, i + by) for i in range(devices) if 0 <= i + by < devices]
    return lax.ppermute(shard, axis, pairs)


def fold_block(partial_value, block_kv, offset, query_heads, query_pos):
    key_part, value_part = block_kv
    piece_len = key_part.shape[0]
    heads_here = query_heads.shape[1]

    def compute(current):
        old_max, old_sum, old_acc = current
        key_heads = key_part.reshape(piece_len, heads_here, HD)
        value_heads = value_part.reshape(piece_len, heads_here, HD)
        scores = jnp.einsum(
            "qhd,khd->hqk", query_heads, key_heads, preferred_element_type=jnp.float32
        ) * HD ** (-0.5)
        key_pos = jnp.arange(piece_len, dtype=jnp.int32)
        causal = key_pos[None, :] <= query_pos[:, None]
        scores = jnp.where(causal[None], scores, -1e30)
        new_max = jnp.maximum(old_max, jnp.max(scores, axis=-1))
        weights = jnp.where(causal[None], jnp.exp(scores - new_max[..., None]), 0.0)
        new_sum = jnp.sum(weights, axis=-1)
        update = jnp.einsum(
            "hqk,khd->hqd",
            weights.astype(jnp.bfloat16),
            value_heads,
            preferred_element_type=jnp.float32,
        )
        return (new_max, new_sum, update)

    def passed(current):
        return current

    return lax.cond(offset <= jnp.max(query_pos), compute, passed, partial_value)


def empty_state(heads_here, num_rows):
    return (
        jnp.full((heads_here, num_rows), -1e30, jnp.float32),
        jnp.zeros((heads_here, num_rows), jnp.float32),
        jnp.zeros((heads_here, num_rows, HD), jnp.float32),
    )


def finish(current):
    output = current[2] / current[1][..., None]
    heads_here, num_rows = current[1].shape
    return jnp.transpose(output, (1, 0, 2)).reshape(num_rows, heads_here * HD).astype(jnp.bfloat16)


def shards(latents, stream, queries, key_rows, value_rows, w_mix, w_head):
    tok_rows = queries.shape[0]
    heads_here = queries.shape[1] // HD
    channels = latents.shape[1]
    ctx_count = lax.axis_size("ctx")
    ctx_index = lax.axis_index("ctx")
    row_base = ctx_index * tok_rows
    own_heads = queries.reshape(tok_rows, heads_here, HD)
    own_pos = row_base + jnp.arange(tok_rows, dtype=jnp.int32)
    result_state = fold_block(
        empty_state(heads_here, tok_rows),
        (
            lax.all_gather(key_rows, "ctx", axis=0, tiled=True),
            lax.all_gather(value_rows, "ctx", axis=0, tiled=True),
        ),
        jnp.int32(0),
        own_heads,
        own_pos,
    )
    attended = finish(result_state)
    fsdp_count = lax.axis_size("fsdp")
    fsdp_index = lax.axis_index("fsdp")
    model_width = stream.shape[1]
    share_cols = model_width // fsdp_count
    mixed_part = jnp.dot(
        attended,
        lax.all_gather(w_mix, "ctx", axis=1, tiled=True),
        preferred_element_type=jnp.float32,
    )
    mixed = lax.psum(mixed_part, "fsdp")
    resid = stream.astype(jnp.float32) + mixed
    head_full = lax.all_gather(w_head, "fsdp", axis=0, tiled=True)
    pred = jnp.dot(resid, head_full.astype(jnp.float32), precision=lax.Precision.HIGHEST)
    resid_mine = lax.dynamic_slice_in_dim(resid, fsdp_index * share_cols, share_cols, 1)
    before = shifted(pred[tok_rows - 1 :], "ctx", 1)
    prior = jnp.concatenate([before, pred[:-1]], axis=0)
    shift_part = prior[:, :channels]
    log_scale = prior[:, channels:]
    inverse = jnp.exp(-log_scale)
    white = (latents - shift_part) * inverse
    loss_scale = float(tok_rows * ctx_count) ** (-0.5)
    d_prior = jnp.concatenate([-white * inverse, 1.0 - white * white], axis=1) * loss_scale
    after = shifted(d_prior[:1], "ctx", -1)
    d_pred = jnp.concatenate([d_prior[1:], after], axis=0)
    grad_part = jnp.dot(resid_mine.T, d_pred, precision=lax.Precision.HIGHEST)
    head_grad = lax.psum(grad_part, "ctx")
    piece_rows = tok_rows // ctx_count

    def mirror_step(pieces):
        return lax.all_to_all(pieces, "ctx", split_axis=0, concat_axis=0, tiled=True)

    first_pass = mirror_step(white.reshape(ctx_count, piece_rows, channels))
    second_pass = mirror_step(first_pass[::-1, ::-1])
    flipped = second_pass[::-1].reshape(tok_rows, channels)
    return (flipped, head_grad)


def solution(mesh):
    return jax.shard_map(
        shards,
        mesh=mesh,
        in_specs=(
            P("ctx", None),
            P("ctx", None),
            P("ctx", "fsdp"),
            P("ctx", "fsdp"),
            P("ctx", "fsdp"),
            P("fsdp", "ctx"),
            P("fsdp", None),
        ),
        out_specs=(P("ctx", None), P("fsdp", None)),
        check_vma=False,
    )
```

profile of v0, /device:TPU:2, one launch (start us, length us, event | category | flops | bytes accessed | tf_op | source)
XLA Modules:
  0.0 1053.6 jit_solution(8933292455666120122)
XLA Ops:
  7.2 0.7 all-gather.4.cloned.1.call-update
  7.9 0.7 all-gather.6.cloned.1.call-update
  8.7 0.7 all-gather.8.cloned.1.call-update
  9.4 0.6 fusion.25
  10.7 156.1 %all-gather.4.cloned.1.call-done = bf16[8192,256]{1,0:T(8,128)(2,1)} async-done(((bf16[128,256]{1,0:T(8,128)(2,1)}), bf16[8192,256]{1,0:T(8,128)(2,1)}) %all-gather.4.cloned.1.call-update) | async-done | bytes 4194320 | tf_op jit(solution)/shard_map/all_gather | solution.py:73
  166.8 148.8 %all-gather.6.cloned.1.call-done = bf16[8192,256]{1,0:T(8,128)(2,1)} async-done(((bf16[128,256]{1,0:T(8,128)(2,1)}), bf16[8192,256]{1,0:T(8,128)(2,1)}) %all-gather.6.cloned.1.call-update) | async-done | bytes 4194320 | tf_op jit(solution)/shard_map/all_gather | solution.py:74
  315.6 11.1 %conditional.1 = (f32[2,128]{1,0:T(2,128)S(1)}, f32[2,128,128]{1,2,0:T(8,128)S(1)}) conditional(s32[]{:T(128)} %convert_element_type.20, () %tuple.16, (s32[128]{0:T(128)S(1)}, bf16[128,256]{1,0:T(8,128)(2,1)}, bf16[8192,256]{1,0:T(8,128)(2,1)}, bf16[8192,256]{1,0:T(8,128)(2,1)}) %tuple.17), branch_computations={%region_1.0_spmd, %region_2.5_spmd} | conditional | flops 1093664512 | bytes 37952016 | solution.py:44
  315.6 0.7 iota_compare_fusion
  316.3 4.0 fusion.27
  320.3 4.2 fusion.3
  324.6 2.1 fusion.2
  326.8 128.6 %all-gather.8.cloned.1.call-done = bf16[256,3072]{0,1:T(8,128)(2,1)} async-done(((bf16[256,48]{0,1:T(8,128)(2,1)}), bf16[256,3072]{0,1:T(8,128)(2,1)}) %all-gather.8.cloned.1.call-update) | async-done | bytes 1572880 | tf_op jit(solution)/shard_map/all_gather | solution.py:87
  455.4 3.2 fusion.28
  458.6 29.8 %all_gather.15 = bf16[3072,128]{1,0:T(8,128)(2,1)S(1)} all-gather(bf16[384,128]{1,0:T(8,128)(2,1)S(1)} %copy-done.1), channel_id=1, replica_groups=mesh['fsdp'=8,'ctx'=64] {'fsdp'}, dimensions={0}, use_global_device_ids=true | all-gather | bytes 884736 | tf_op jit(solution)/shard_map/all_gather | solution.py:92
  488.5 59.2 %all-reduce.3.cloned.1.call-done = f32[128,3072]{1,0:T(8,128)} async-done(((f32[128,3072]{1,0:T(8,128)}), f32[128,3072]{1,0:T(8,128)}) %all-reduce.3.cloned.1.call-update) | async-done | bytes 1572880 | tf_op jit(solution)/shard_map/psum | solution.py:90
  547.7 1.6 convert_add_fusion
  549.3 0.9 fusion.29
  550.2 1.3 collective-permute-start
  551.6 0.7 collective-permute-done
  552.5 1.3 collective-permute-start.1
  553.8 0.7 reshape.46
  554.5 19.8 %all-to-all-start = ((f32[64,1,128]{2,1,0:T(1,128)}), f32[64,1,128]{2,1,0:T(1,128)S(1)}, u32[]{:S(2)}, u32[]{:S(2)}) async-start(f32[64,1,128]{2,1,0:T(1,128)} %reshape.46), calls=%async_computation | async-start | bytes 65536 | tf_op jit(solution)/shard_map/all_to_all | solution.py:110
  574.5 1.2 fusion.15
  575.7 13.6 %all-to-all-done = f32[64,1,128]{2,1,0:T(1,128)S(1)} async-done(((f32[64,1,128]{2,1,0:T(1,128)}), f32[64,1,128]{2,1,0:T(1,128)S(1)}, u32[]{:S(2)}, u32[]{:S(2)}) %all-to-all-start) | async-done | bytes 32800 | tf_op jit(solution)/shard_map/all_to_all | solution.py:110
  589.2 0.5 broadcast.19
  589.7 0.7 reduce
  590.6 0.1 rev.6
  590.8 18.6 %all_to_all.10 = f32[64,1,128]{2,1,0:T(1,128)S(1)} all-to-all(f32[64,1,128]{2,1,0:T(1,128)S(1)} %reshape.48), channel_id=1, replica_groups=mesh['fsdp'=8,'ctx'=64] {'ctx'}, dimensions={0} | all-to-all | bytes 65536 | tf_op jit(solution)/shard_map/all_to_all | solution.py:110
  609.5 0.7 reduce.1
  610.3 0.7 copy.20
  611.0 434.5 %all-reduce.5.cloned.1.call-done = f32[384,128]{1,0:T(8,128)} async-done(((f32[384,128]{1,0:T(8,128)}), f32[384,128]{1,0:T(8,128)}) %all-reduce.5.cloned.1.call-update) | async-done | bytes 196624 | tf_op jit(solution)/shard_map/psum | solution.py:106
  1045.5 1.6 copy.48
  (28 shorter events, 0.9 us)
Async XLA Ops:
  7.2 159.7 %all-gather.4.cloned.1.call-start = ((), (), s32[]{:S(2)}) async-start(), calls=%async_computation.2 | async-start | bytes 4259840 | tf_op jit(solution)/shard_map/all_gather | solution.py:73
  7.9 307.7 %all-gather.6.cloned.1.call-start = ((), (), s32[]{:S(2)}) async-start(), calls=%async_computation.3 | async-start | bytes 4259840 | tf_op jit(solution)/shard_map/all_gather | solution.py:74
  8.6 446.7 %all-gather.8.cloned.1.call-start = ((), (), s32[]{:S(2)}) async-start(), calls=%async_computation.4 | async-start | bytes 1597440 | tf_op jit(solution)/shard_map/all_gather | solution.py:87
  9.4 538.3 %all-reduce.3.cloned.1.call-start = ((), (), s32[]{:S(2)}) async-start(), calls=%async_computation.5 | async-start | bytes 3145728 | tf_op jit(solution)/shard_map/psum | solution.py:90
  326.7 131.9 %copy-start.1 = (bf16[384,128]{1,0:T(8,128)(2,1)S(1)}, bf16[384,128]{1,0:T(8,128)(2,1)}, u32[]{:S(2)}) copy-start(bf16[384,128]{1,0:T(8,128)(2,1)} %param.15) | copy-start | bytes 294916
  326.7 221.0 %copy-start = (bf16[128,3072]{1,0:T(8,128)(2,1)S(1)}, bf16[128,3072]{1,0:T(8,128)(2,1)}, u32[]{:S(2)}) copy-start(bf16[128,3072]{1,0:T(8,128)(2,1)} %param.10) | copy-start | bytes 2359300
  458.6 92.9 %copy-start.2 = (f32[128,64]{0,1:T(8,128)S(1)}, f32[128,64]{0,1:T(8,128)}, u32[]{:S(2)}) copy-start(f32[128,64]{0,1:T(8,128)} %param.9) | copy-start | bytes 98308
  550.2 2.1 collective-permute-start
  552.5 22.0 %collective-permute-start.1 = (f32[1,128]{1,0:T(1,128)S(1)}, f32[1,128]{1,0:T(1,128)S(1)}, u32[]{:S(2)}, u32[]{:S(2)}) collective-permute-start(f32[1,128]{1,0:T(1,128)S(1)} %slice.29), channel_id=1, source_target_pairs={{1,0},{2,1},{3,2},{4,3},{5,4},{6,5},{7,6},{8,7},{9,8},{10,9},{11,1... | collective-permute-start | bytes 1544 | tf_op jit(solution)/shard_map/ppermute | solution.py:12
  554.5 34.7 %all-to-all-start = ((f32[64,1,128]{2,1,0:T(1,128)}), f32[64,1,128]{2,1,0:T(1,128)S(1)}, u32[]{:S(2)}, u32[]{:S(2)}) async-start(f32[64,1,128]{2,1,0:T(1,128)} %reshape.46), calls=%async_computation | async-start | bytes 65536 | tf_op jit(solution)/shard_map/all_to_all | solution.py:110
  574.4 471.1 %all-reduce.5.cloned.1.call-start = ((), (), s32[]{:S(2)}) async-start(), calls=%async_computation.6 | async-start | bytes 393216 | tf_op jit(solution)/shard_map/psum | solution.py:106
Sparse Core Ops, SparseCore 0:
  11.3 155.4 all-gather.3
  170.1 145.4 all-gather.5
  318.9 136.4 all-gather.7
  458.7 88.9 all-reduce.2
  578.4 467.0 all-reduce.4
where the time goes:
time: 1050 us
  waiting for transfers between devices  944 us (90%)
  blocking collectives  48.5 us (5%)
  starting transfers between devices  22.6 us (2%)
  between operations  14.6 us (1%)
  matrix products  13.5 us (1%)
    psum x1, waiting for transfers between devices, shards(): head_grad = lax.psum(grad_part, 'ctx')  434 us
    all_gather x1, waiting for transfers between devices, shards(): lax.all_gather(key_rows, 'ctx', axis=0, tiled=True)  156 us
    all_gather x1, waiting for transfers between devices, shards(): lax.all_gather(value_rows, 'ctx', axis=0, tiled=True)  149 us
    all_gather x1, waiting for transfers between devices, shards(): lax.all_gather(w_mix, 'ctx', axis=1, tiled=True)  129 us
    psum x1, waiting for transfers between devices, shards(): mixed = lax.psum(mixed_part, 'fsdp')  59.2 us
    all_gather x1, blocking collectives, shards(): head_full = lax.all_gather(w_head, 'fsdp', axis=0, tiled=True)  29.8 us
  transfers between devices with their start and end apart: 8, of which 7 were waited for; matrix products, arithmetic and copies ran while one was open for 2% of the time, Pallas kernels for 0%

commit v1 on v0

--- a/solution.py
+++ b/solution.py
@@ -103,7 +103,7 @@
     after = shifted(d_prior[:1], "ctx", -1)
     d_pred = jnp.concatenate([d_prior[1:], after], axis=0)
     grad_part = jnp.dot(resid_mine.T, d_pred, precision=lax.Precision.HIGHEST)
-    head_grad = lax.psum(grad_part, "ctx")
+    head_grad = jnp.sum(lax.all_gather(grad_part, "ctx"), axis=0)
     piece_rows = tok_rows // ctx_count
 
     def mirror_step(pieces):

time: 1050 us -> 757 us (0.72)
  the two profiles are of different devices: /device:TPU:2 before, /device:TPU:1 now
where the time goes in v1:
time: 757 us; the launch traced here: 756 us
  waiting for transfers between devices  629 us (83%)
  blocking collectives  74.6 us (10%)
  between operations  14.6 us (2%)
  matrix products  13.5 us (2%)
  other arithmetic  12.5 us (2%)
  starting transfers between devices  10.1 us (1%)
    all_gather x1, waiting for transfers between devices, shards(): lax.all_gather(key_rows, 'ctx', axis=0, tiled=True)  157 us
    all_gather x1, waiting for transfers between devices, shards(): lax.all_gather(value_rows, 'ctx', axis=0, tiled=True)  149 us
    all_gather x1, waiting for transfers between devices, shards(): lax.all_gather(w_mix, 'ctx', axis=1, tiled=True)  129 us
    all_gather x1, waiting for transfers between devices, shards(): head_grad = jnp.sum(lax.all_gather(grad_part, 'ctx'), axis=0)  128 us
    psum x1, waiting for transfers between devices, shards(): mixed = lax.psum(mixed_part, 'fsdp')  60.2 us
    all_to_all x2, blocking collectives, mirror_step(): lax.all_to_all(pieces, 'ctx', split_axis=0, concat_axis=0, tiled=True)  48.8 us
    all_gather x1, blocking collectives, shards(): head_full = lax.all_gather(w_head, 'fsdp', axis=0, tiled=True)  25.8 us
  transfers between devices with their start and end apart: 7, of which 7 were waited for; matrix products, arithmetic and copies ran while one was open for 2% of the time, Pallas kernels for 0%

profile of v1, /device:TPU:1, one launch (start us, length us, event | category | flops | bytes accessed | tf_op | source)
XLA Modules:
  0.0 756.2 jit_solution(14364974631560226811)
XLA Ops:
  7.2 0.7 all-gather.6.cloned.1.call-update
  7.9 0.7 all-gather.8.cloned.1.call-update
  8.7 0.7 all-gather.10.cloned.1.call-update
  9.4 0.6 fusion.25
  10.7 157.4 %all-gather.6.cloned.1.call-done = bf16[8192,256]{1,0:T(8,128)(2,1)} async-done(((bf16[128,256]{1,0:T(8,128)(2,1)}), bf16[8192,256]{1,0:T(8,128)(2,1)}) %all-gather.6.cloned.1.call-update) | async-done | bytes 4194320 | tf_op jit(solution)/shard_map/all_gather | solution.py:73
  168.1 148.8 %all-gather.8.cloned.1.call-done = bf16[8192,256]{1,0:T(8,128)(2,1)} async-done(((bf16[128,256]{1,0:T(8,128)(2,1)}), bf16[8192,256]{1,0:T(8,128)(2,1)}) %all-gather.8.cloned.1.call-update) | async-done | bytes 4194320 | tf_op jit(solution)/shard_map/all_gather | solution.py:74
  316.9 11.1 %conditional.1 = (f32[2,128]{1,0:T(2,128)S(1)}, f32[2,128,128]{1,2,0:T(8,128)S(1)}) conditional(s32[]{:T(128)} %convert_element_type.20, () %tuple.16, (s32[128]{0:T(128)S(1)}, bf16[128,256]{1,0:T(8,128)(2,1)}, bf16[8192,256]{1,0:T(8,128)(2,1)}, bf16[8192,256]{1,0:T(8,128)(2,1)}) %tuple.17), branch_computations={%region_1.0_spmd, %region_2.5_spmd} | conditional | flops 1093664512 | bytes 37952016 | solution.py:44
  316.9 0.7 iota_compare_fusion
  317.6 4.0 fusion.27
  321.6 4.2 fusion.3
  325.9 2.1 fusion.2
  328.0 128.6 %all-gather.10.cloned.1.call-done = bf16[256,3072]{0,1:T(8,128)(2,1)} async-done(((bf16[256,48]{0,1:T(8,128)(2,1)}), bf16[256,3072]{0,1:T(8,128)(2,1)}) %all-gather.10.cloned.1.call-update) | async-done | bytes 1572880 | tf_op jit(solution)/shard_map/all_gather | solution.py:87
  456.7 3.2 fusion.28
  460.0 25.8 %all_gather.21 = bf16[3072,128]{1,0:T(8,128)(2,1)S(1)} all-gather(bf16[384,128]{1,0:T(8,128)(2,1)S(1)} %copy-done.1), channel_id=1, replica_groups=mesh['fsdp'=8,'ctx'=64] {'fsdp'}, dimensions={0}, use_global_device_ids=true | all-gather | bytes 884736 | tf_op jit(solution)/shard_map/all_gather | solution.py:92
  485.7 60.2 %all-reduce.2.cloned.1.call-done = f32[128,3072]{1,0:T(8,128)} async-done(((f32[128,3072]{1,0:T(8,128)}), f32[128,3072]{1,0:T(8,128)}) %all-reduce.2.cloned.1.call-update) | async-done | bytes 1572880 | tf_op jit(solution)/shard_map/psum | solution.py:90
  546.0 1.6 convert_add_fusion
  547.5 0.9 fusion.29
  548.4 8.0 %collective-permute-start = (f32[1,128]{1,0:T(1,128)S(1)}, f32[1,128]{1,0:T(1,128)S(1)}, u32[]{:S(2)}, u32[]{:S(2)}) collective-permute-start(f32[1,128]{1,0:T(1,128)S(1)} %slice.24), channel_id=1, source_target_pairs={{0,1},{1,2},{2,3},{3,4},{4,5},{5,6},{6,7},{7,8},{8,9},{9,10},{10,1... | collective-permute-start | bytes 1544 | tf_op jit(solution)/shard_map/ppermute | solution.py:12
  556.5 0.6 collective-permute-done
  557.3 1.9 collective-permute-start.1
  559.3 3.4 collective-permute-done.1
  562.7 1.2 fusion.15
  563.9 0.1 reshape.47
  564.0 29.8 %all_to_all.10 = f32[64,1,128]{2,1,0:T(1,128)S(1)} all-to-all(f32[64,1,128]{2,1,0:T(1,128)S(1)} %reshape.47), channel_id=1, replica_groups=mesh['fsdp'=8,'ctx'=64] {'ctx'}, dimensions={0} | all-to-all | bytes 65536 | tf_op jit(solution)/shard_map/all_to_all | solution.py:110
  593.8 0.5 broadcast.19
  594.3 0.7 reduce
  595.1 0.1 rev.6
  595.4 19.0 %all_to_all.11 = f32[64,1,128]{2,1,0:T(1,128)S(1)} all-to-all(f32[64,1,128]{2,1,0:T(1,128)S(1)} %reshape.49), channel_id=1, replica_groups=mesh['fsdp'=8,'ctx'=64] {'ctx'}, dimensions={0} | all-to-all | bytes 65536 | tf_op jit(solution)/shard_map/all_to_all | solution.py:110
  614.5 0.7 reduce.1
  615.3 0.7 copy.20
  616.0 127.8 %all-gather.12.cloned.1.call-done = f32[24576,128]{1,0:T(8,128)} async-done(((f32[384,128]{1,0:T(8,128)}), f32[24576,128]{1,0:T(8,128)}) %all-gather.12.cloned.1.call-update) | async-done | bytes 12582928 | tf_op jit(solution)/shard_map/all_gather | solution.py:106
  743.8 5.8 reduce_sum.18
  (27 shorter events, 0.9 us)
Async XLA Ops:
  7.2 160.9 %all-gather.6.cloned.1.call-start = ((), (), s32[]{:S(2)}) async-start(), calls=%async_computation.2 | async-start | bytes 4259840 | tf_op jit(solution)/shard_map/all_gather | solution.py:73
  7.9 309.0 %all-gather.8.cloned.1.call-start = ((), (), s32[]{:S(2)}) async-start(), calls=%async_computation.3 | async-start | bytes 4259840 | tf_op jit(solution)/shard_map/all_gather | solution.py:74
  8.6 448.0 %all-gather.10.cloned.1.call-start = ((), (), s32[]{:S(2)}) async-start(), calls=%async_computation.4 | async-start | bytes 1597440 | tf_op jit(solution)/shard_map/all_gather | solution.py:87
  9.4 536.6 %all-reduce.2.cloned.1.call-start = ((), (), s32[]{:S(2)}) async-start(), calls=%async_computation.5 | async-start | bytes 3145728 | tf_op jit(solution)/shard_map/psum | solution.py:90
  328.0 132.0 %copy-start.1 = (bf16[384,128]{1,0:T(8,128)(2,1)S(1)}, bf16[384,128]{1,0:T(8,128)(2,1)}, u32[]{:S(2)}) copy-start(bf16[384,128]{1,0:T(8,128)(2,1)} %param.15) | copy-start | bytes 294916
  328.0 218.0 %copy-start = (bf16[128,3072]{1,0:T(8,128)(2,1)S(1)}, bf16[128,3072]{1,0:T(8,128)(2,1)}, u32[]{:S(2)}) copy-start(bf16[128,3072]{1,0:T(8,128)(2,1)} %param.10) | copy-start | bytes 2359300
  459.9 96.5 %copy-start.2 = (f32[128,64]{0,1:T(8,128)S(1)}, f32[128,64]{0,1:T(8,128)}, u32[]{:S(2)}) copy-start(f32[128,64]{0,1:T(8,128)} %param.9) | copy-start | bytes 98308
  459.9 283.9 %all-gather.12.cloned.1.call-start = ((), (), s32[]{:S(2)}) async-start(), calls=%async_computation.6 | async-start | bytes 12779520 | tf_op jit(solution)/shard_map/all_gather | solution.py:106
  548.4 8.7 %collective-permute-start = (f32[1,128]{1,0:T(1,128)S(1)}, f32[1,128]{1,0:T(1,128)S(1)}, u32[]{:S(2)}, u32[]{:S(2)}) collective-permute-start(f32[1,128]{1,0:T(1,128)S(1)} %slice.24), channel_id=1, source_target_pairs={{0,1},{1,2},{2,3},{3,4},{4,5},{5,6},{6,7},{7,8},{8,9},{9,10},{10,1... | collective-permute-start | bytes 1544 | tf_op jit(solution)/shard_map/ppermute | solution.py:12
  557.3 5.4 collective-permute-start.1
Sparse Core Ops, SparseCore 0:
  11.3 156.7 all-gather.5
  171.4 145.4 all-gather.7
  320.2 136.4 all-gather.9
  460.0 85.8 all-reduce.1
  564.0 179.7 all-gather.11
